TPU v7x, 128 devices: a whole 4x4x4 slice. The times are simulated.
128 devices in a mesh: tok: 8 (over y, x_lo), tp: 16 (over z, x_hi, core).
Axes of the slice: x: 4 (x_hi: 2, x_lo: 2; x = x_hi * 2 + x_lo), y: 4, z: 4, core: 2. Of those that a mesh axis runs over, the one named last changes fastest.
Arguments:
- source: bfloat16 [2048, 8192], P('tp', 'tok'), may hold values from -6 to 6
- row_token: int32 [2048], replicated, may hold values from 0 to 2047, each once
- seg_ids: int32 [8, 256], P('tok'), may hold values from 0 to 3, never falling along the last dimension, each value on 1 to 128 neighbouring positions
- stitch_weight: bfloat16 [8192, 8192], P('tok', 'tp'), may hold values from -0.0625 to 0.0625
- norm_gain: float32 [8192], replicated, may hold values from 0.5 to 1.5
- q_weight: bfloat16 [8192, 8192], P(None, 'tp'), may hold values from -2 to 2
- kv_weight: bfloat16 [8192, 2048], P(None, 'tp'), may hold values from -2 to 2
- o_weight: bfloat16 [8192, 8192], P('tp'), may hold values from -0.0625 to 0.0625
- out_grad: bfloat16 [2048, 8192], P('tok', 'tp'), may hold values from -6 to 6
Outputs:
- layer_out: bfloat16 [2048, 8192], P('tok', 'tp')
- stitch_grad: float32 [8192, 8192], P('tok', 'tp')
Inputs may be any that keep to these rules, and one draw needn't show every extreme that they name: `row_token`: each token index appears exactly once. `seg_ids`: within a pack the ids never fall; a document holds 1 to 128 tokens.
All inputs are finite; a program needn't handle non-finite values.
Results may differ from a plain program's by a relative error of at most 0.024.
Values may be sent and summed in bfloat16 or wider, within the bound.
A program may use at most 128 MiB of HBM per device.

v0:
```python
import math
import jax
import jax.numpy as jnp
from jax import lax
from jax.sharding import PartitionSpec as P

HD = 128
epsilon = 1e-05


def swapped(value, axis, distance):
    mask = 2**distance
    pairs = [(source, source ^ mask) for source in range(lax.axis_size(axis))]
    return lax.ppermute(value, axis, pairs)


def frequencies():
    exponent = jnp.arange(0, HD, 2).astype(jnp.float32) / HD
    plain_rate = 500000.0 ** (-exponent)
    wavelength = 2.0 * math.pi / plain_rate
    smoothing = (8192.0 / wavelength - 1.0) / 3.0
    blended = (1.0 - smoothing) * plain_rate / 8.0 + smoothing * plain_rate
    return jnp.where(
        wavelength < 2048.0, plain_rate, jnp.where(wavelength > 8192.0, plain_rate / 8.0, blended)
    )


def rotate(vector_in, cosine_table, sine_table):
    half_size = vector_in.shape[-1] // 2
    first_half = vector_in[..., :half_size]
    second = vector_in[..., half_size:]
    return jnp.concatenate(
        [
            first_half * cosine_table - second * sine_table,
            second * cosine_table + first_half * sine_table,
        ],
        axis=-1,
    )


def unrotate(vector_in, cosine_table, sine_table):
    half_size = vector_in.shape[-1] // 2
    first_half = vector_in[..., :half_size]
    second = vector_in[..., half_size:]
    return jnp.concatenate(
        [
            first_half * cosine_table + second * sine_table,
            second * cosine_table - first_half * sine_table,
        ],
        axis=-1,
    )


def body(
    source, row_token, seg_ids, stitch_weight, norm_gain, q_weight, kv_weight, o_weight, out_grad
):
    tp_rank = lax.axis_index("tp")
    pack_len = seg_ids.shape[1]
    score_scale = 1.0 / math.sqrt(HD)
    gathered = lax.all_gather(source, "tp", axis=0, tiled=True)
    every_row_stack = gathered.shape[0]
    placing = (
        jnp.zeros((every_row_stack,), jnp.int32)
        .at[row_token]
        .set(jnp.arange(every_row_stack, dtype=jnp.int32))
    )
    column_block = jnp.take(gathered, placing, axis=0)
    token_rows = lax.all_to_all(column_block, "tok", split_axis=0, concat_axis=1, tiled=True)
    features = token_rows
    hidden_cols = jnp.dot(
        features,
        lax.all_gather(stitch_weight, "tok", axis=0, tiled=True),
        preferred_element_type=jnp.float32,
    )
    hidden_bf = hidden_cols.astype(jnp.bfloat16)
    hidden_all = lax.all_gather(hidden_bf, "tp", axis=1, tiled=True)
    hidden_f = hidden_all.astype(jnp.float32)
    inv_rms = lax.rsqrt(jnp.mean(hidden_f * hidden_f, axis=1, keepdims=True) + epsilon)
    normed = (hidden_f * inv_rms * norm_gain).astype(jnp.bfloat16)
    seg_row = seg_ids[0]
    earlier = jnp.sum((seg_row[None, :] < seg_row[:, None]).astype(jnp.int32), axis=1)
    index_row = jnp.arange(pack_len, dtype=jnp.int32)
    angles = (index_row - earlier).astype(jnp.float32)[:, None] * frequencies()[None, :]
    cosines = jnp.cos(angles)[:, None, :]
    sine_table = jnp.sin(angles)[:, None, :]
    allowed = (
        (seg_row[:, None] == seg_row[None, :]) & (index_row[None, :] <= index_row[:, None])
    ).astype(jnp.int32)
    local_heads = q_weight.shape[1] // HD
    kv_local = 1
    repeat = local_heads // kv_local
    queries = rotate(
        jnp.dot(normed, q_weight, preferred_element_type=jnp.float32).reshape(
            pack_len, local_heads, HD
        ),
        cosines,
        sine_table,
    ).astype(jnp.bfloat16)
    projected = jnp.dot(normed, kv_weight, preferred_element_type=jnp.float32)
    is_key = tp_rank % 2 == 0
    own_part = jnp.where(
        is_key, rotate(projected, cosines[:, 0], sine_table[:, 0]), projected
    ).astype(jnp.bfloat16)
    partner = swapped(own_part, "tp", 0)
    per_head_keys = jnp.where(is_key, own_part, partner)[:, None, :]
    per_head_values = jnp.where(is_key, partner, own_part)[:, None, :]
    per_head_queries = queries.reshape(pack_len, kv_local, repeat, HD)
    scores = (
        jnp.einsum(
            "nkej,wkj->kenw", per_head_queries, per_head_keys, preferred_element_type=jnp.float32
        )
        * score_scale
    )
    scores = jnp.where(allowed != 0, scores, -1e30)
    row_max = jnp.max(scores, axis=-1, keepdims=True)
    exponents = jnp.exp(scores - row_max)
    attention = exponents / jnp.sum(exponents, axis=-1, keepdims=True)
    attention_half_precision = attention.astype(jnp.bfloat16)
    context = jnp.einsum(
        "cnfo,och->fcnh",
        attention_half_precision,
        per_head_values,
        preferred_element_type=jnp.float32,
    ).astype(jnp.bfloat16)
    context = context.reshape(pack_len, local_heads * HD)
    attended = lax.psum_scatter(
        jnp.dot(context, o_weight, preferred_element_type=jnp.float32).astype(jnp.bfloat16),
        "tp",
        scatter_dimension=1,
        tiled=True,
    ).astype(jnp.float32)
    layer_out = (hidden_bf.astype(jnp.float32) + attended).astype(jnp.bfloat16)
    gradient_every_row = lax.all_gather(out_grad, "tp", axis=1, tiled=True)
    grad_context = jnp.dot(
        gradient_every_row, o_weight.T, preferred_element_type=jnp.float32
    ).astype(jnp.bfloat16)
    context_gradient = grad_context.reshape(pack_len, kv_local, repeat, HD)
    grad_probs = jnp.einsum(
        "nkej,wkj->kenw", context_gradient, per_head_values, preferred_element_type=jnp.float32
    )
    centered = grad_probs - jnp.sum(grad_probs * attention, axis=-1, keepdims=True)
    score_gradient = (attention * centered * score_scale).astype(jnp.bfloat16)
    query_grad = jnp.einsum(
        "cnfo,och->fcnh", score_gradient, per_head_keys, preferred_element_type=jnp.float32
    )
    grad_queries = unrotate(
        query_grad.reshape(pack_len, local_heads, HD), cosines, sine_table
    ).astype(jnp.bfloat16)
    key_part = jnp.einsum(
        "bwlf,lbwj->fbj", score_gradient, per_head_queries, preferred_element_type=jnp.float32
    )
    value_part = jnp.einsum(
        "bwlf,lbwj->fbj",
        attention_half_precision,
        context_gradient,
        preferred_element_type=jnp.float32,
    )
    outgoing = jnp.where(is_key, value_part, key_part)[:, 0]
    incoming = swapped(outgoing.astype(jnp.bfloat16), "tp", 0).astype(outgoing.dtype)
    own_sum = jnp.where(is_key, key_part, value_part)[:, 0] + incoming
    grad_pairs = jnp.where(
        is_key, unrotate(own_sum, cosines[:, 0], sine_table[:, 0]), own_sum
    ).astype(jnp.bfloat16)
    grad_normed = jnp.dot(
        grad_queries.reshape(pack_len, local_heads * HD),
        q_weight.T,
        preferred_element_type=jnp.float32,
    )
    grad_normed = grad_normed + jnp.dot(grad_pairs, kv_weight.T, preferred_element_type=jnp.float32)
    weighted = norm_gain * grad_normed
    cubed = inv_rms * inv_rms * inv_rms
    norm_term = inv_rms * weighted - hidden_f * cubed * jnp.mean(
        weighted * hidden_f, axis=1, keepdims=True
    )
    grad_sum = lax.psum_scatter(
        norm_term.astype(jnp.bfloat16), "tp", scatter_dimension=1, tiled=True
    ).astype(jnp.float32)
    grad_hidden = (out_grad.astype(jnp.float32) + grad_sum).astype(jnp.bfloat16)
    features = token_rows
    stitch_grad = lax.psum_scatter(
        lax.dot_general(
            features, grad_hidden, (((0,), (0,)), ((), ())), preferred_element_type=jnp.float32
        ).astype(jnp.bfloat16),
        "tok",
        scatter_dimension=0,
        tiled=True,
    ).astype(jnp.float32)
    return (layer_out, stitch_grad)


def solution(mesh):
    placed = (
        P("tp", "tok"),
        P(),
        P("tok", None),
        P("tok", "tp"),
        P(),
        P(None, "tp"),
        P(None, "tp"),
        P("tp", None),
        P("tok", "tp"),
    )
    return jax.shard_map(
        body,
        mesh=mesh,
        in_specs=placed,
        out_specs=(P("tok", "tp"), P("tok", "tp")),
        check_vma=False,
    )
```

profile of v0, /device:TPU:1, one launch (start us, length us, event | category | flops | bytes accessed | tf_op | source)
XLA Modules:
  0.0 783.7 jit_solution(5317935610867189701)
XLA Ops:
  7.2 0.0 all-gather.5.cloned.1.call-start
  7.2 0.7 all-gather.5.cloned.1.call-update
  7.9 0.0 all-gather.7.cloned.1.call-start
  8.0 0.7 all-gather.7.cloned.1.call-update
  8.7 0.0 all-gather.11.cloned.1.call-start
  8.7 0.7 all-gather.11.cloned.1.call-update
  9.4 0.0 all-gather.9.cloned.1.call-start
  9.4 0.7 compare_select_fusion.1
  10.1 8.0 %scatter_custom_fusion = s32[2048]{0:T(1024)S(1)} fusion(s32[2048]{0:T(1024)S(1)} %compare_select_fusion.1, s32[2048]{0:T(1024)S(1)} %iota.19, s32[]{:T(128)} %constant.22.clone.1), kind=kCustom, calls=%fused_computation.84 | custom fusion | bytes 8196 | tf_op jit(solution)/shard_map/scatter | solution.py:65
  18.2 51.3 %all-gather.5.cloned.1.call-done = bf16[2048,1024]{1,0:T(8,128)(2,1)} async-done(((bf16[128,1024]{1,0:T(8,128)(2,1)}), bf16[2048,1024]{1,0:T(8,128)(2,1)}) %all-gather.5.cloned.1.call-update) | async-done | bytes 4194320 | tf_op jit(solution)/shard_map/all_gather | solution.py:60
  69.6 13.6 %gather_fusion = bf16[2048,1024]{1,0:T(8,128)(2,1)} fusion(bf16[2048,1024]{1,0:T(8,128)(2,1)} %all-gather.5.cloned.1.call-done, s32[2048]{0:T(1024)S(1)} %fusion.43), kind=kCustom, calls=%fused_computation | custom fusion | bytes 8396800 | tf_op jit(solution)/shard_map/jit(_take)/gather | solution.py:67
  83.2 6.4 copy.25
  89.7 2.6 broadcast_select_fusion
  92.3 98.4 %all_to_all.16 = bf16[8,256,1024]{1,2,0:T(8,128)(2,1)} all-to-all(bf16[8,256,1024]{1,2,0:T(8,128)(2,1)S(1)} %broadcast_select_fusion), channel_id=1, replica_groups=mesh['tok'=8,'tp'=16] {'tok'}, dimensions={0} | all-to-all | bytes 8388608 | tf_op jit(solution)/shard_map/all_to_all | solution.py:68
  190.7 91.1 %all-gather.7.cloned.1.call-done = bf16[8192,512]{1,0:T(8,128)(2,1)} async-done(((bf16[1024,512]{1,0:T(8,128)(2,1)}), bf16[8192,512]{1,0:T(8,128)(2,1)}) %all-gather.7.cloned.1.call-update) | async-done | bytes 8388624 | tf_op jit(solution)/shard_map/all_gather | solution.py:72
  281.8 7.7 convolution_convert_fusion.4
  289.6 0.0 all-gather.9.cloned.1.call-update
  289.6 0.0 reduce-scatter.6.cloned.1.call-start
  289.7 0.1 convert_reduce_fusion
  289.8 0.3 multiply_cosine_fusion
  290.1 0.1 copy.27
  290.2 0.1 copy.29
  290.3 0.7 convert_compare_fusion
  291.0 51.5 %all-gather.11.cloned.1.call-done = bf16[256,8192]{1,0:T(8,128)(2,1)} async-done(((bf16[256,512]{1,0:T(8,128)(2,1)}), bf16[256,8192]{1,0:T(8,128)(2,1)}) %all-gather.11.cloned.1.call-update) | async-done | bytes 4194320 | tf_op jit(solution)/shard_map/all_gather | solution.py:133
  342.6 7.0 convolution_convert_fusion.3
  349.6 0.8 copy.53
  350.4 49.4 %all-gather.9.cloned.1.call-done = bf16[256,8192]{1,0:T(8,128)(2,1)} async-done(((bf16[256,512]{1,0:T(8,128)(2,1)}), bf16[256,8192]{1,0:T(8,128)(2,1)}) %all-gather.9.cloned.1.call-update) | async-done | bytes 4194320 | tf_op jit(solution)/shard_map/all_gather | solution.py:76
  399.9 3.3 fusion.1
  403.1 0.6 multiply_multiply_fusion
  403.7 3.9 fusion.12
  407.6 0.3 fusion.32
  408.0 0.5 collective-permute-start
  408.5 5.8 fusion.10
  414.3 0.2 reshape.193
  414.5 0.3 fusion.51
  414.9 0.1 subtract_convert_fusion.1
  415.0 1.3 fusion.52
  416.3 0.2 fusion.15
  416.5 1.9 convolution_bitcast_fusion.2
  418.5 0.3 multiply_reduce_fusion
  418.8 0.3 fusion.16
  419.1 0.4 convolution_bitcast_fusion.3
  419.5 1.2 convolution_bitcast_fusion.1
  420.7 0.3 add_convert_fusion.1
  421.0 0.9 pad_maximum_fusion.1
  421.8 1.1 copy.36
  423.0 1.3 collective-permute-start.1
  424.2 5.9 fusion.53
  430.2 0.3 fusion.34
  430.6 5.3 fusion.7
  435.9 5.9 fusion.6
  441.8 0.0 reduce-scatter.6.cloned.1.call-update
  441.8 0.3 reduce-scatter.4.cloned.1.call-start
  442.1 0.3 convolution_convert_fusion.2
  442.4 7.7 convolution_convert_fusion.1
  450.2 0.0 reduce-scatter.4.cloned.1.call-update
  450.2 0.0 reduce-scatter.8.cloned.1.call-start
  450.3 68.1 %reduce-scatter.6.cloned.1.call-done = bf16[256,512]{1,0:T(8,128)(2,1)} async-done(((bf16[256,8192]{1,0:T(8,128)(2,1)}), bf16[256,512]{1,0:T(8,128)(2,1)}) %reduce-scatter.6.cloned.1.call-update) | async-done | bytes 262160 | tf_op jit(solution)/shard_map/reduce_scatter | solution.py:175
  518.4 7.8 convolution_convert_fusion
  526.2 0.0 reduce-scatter.8.cloned.1.call-update
  526.2 76.0 %reduce-scatter.4.cloned.1.call-done = bf16[256,512]{1,0:T(8,128)(2,1)} async-done(((bf16[256,8192]{1,0:T(8,128)(2,1)}), bf16[256,512]{1,0:T(8,128)(2,1)}) %reduce-scatter.4.cloned.1.call-update) | async-done | bytes 262160 | tf_op jit(solution)/shard_map/reduce_scatter | solution.py:126
  602.2 1.7 add_convert_fusion.2
  604.0 170.1 %reduce-scatter.8.cloned.1.call-done = bf16[1024,512]{1,0:T(8,128)(2,1)} async-done(((bf16[8192,512]{1,0:T(8,128)(2,1)}), bf16[1024,512]{1,0:T(8,128)(2,1)}) %reduce-scatter.8.cloned.1.call-update) | async-done | bytes 1048592 | tf_op jit(solution)/shard_map/reduce_scatter | solution.py:180
  774.0 2.8 convert_element_type.137
  (46 shorter events, 0.2 us)
Async XLA Ops:
  7.2 396.5 %copy-start = (bf16[8192,128]{1,0:T(8,128)(2,1)S(1)}, bf16[8192,128]{1,0:T(8,128)(2,1)}, u32[]{:S(2)}) copy-start(bf16[8192,128]{1,0:T(8,128)(2,1)} %param.15) | copy-start | bytes 6291460
  7.2 62.4 %all-gather.5.cloned.1.call-start = ((), (), s32[]{:S(2)}) async-start(), calls=%async_computation.4 | async-start | bytes 4456448 | tf_op jit(solution)/shard_map/all_gather | solution.py:60
  7.9 273.9 %all-gather.7.cloned.1.call-start = ((), (), s32[]{:S(2)}) async-start(), calls=%async_computation.5 | async-start | bytes 9437184 | tf_op jit(solution)/shard_map/all_gather | solution.py:72
  8.7 333.9 %all-gather.11.cloned.1.call-start = ((), (), s32[]{:S(2)}) async-start(), calls=%async_computation.8 | async-start | bytes 4456448 | tf_op jit(solution)/shard_map/all_gather | solution.py:133
  9.4 390.5 %all-gather.9.cloned.1.call-start = ((), (), s32[]{:S(2)}) async-start(), calls=%async_computation.6 | async-start | bytes 4456448 | tf_op jit(solution)/shard_map/all_gather | solution.py:76
  281.8 7.8 copy-start.13
  289.6 228.8 %reduce-scatter.6.cloned.1.call-start = ((), (), s32[]{:S(2)}) async-start(), calls=%async_computation.9 | async-start | bytes 4456448 | tf_op jit(solution)/shard_map/reduce_scatter | solution.py:175
  291.0 112.6 %copy-start.11 = (f32[8192]{0:T(1024)S(1)}, f32[8192]{0:T(1024)}, u32[]{:S(2)}) copy-start(f32[8192]{0:T(1024)} %param.13) | copy-start | bytes 98308
  399.9 8.6 %copy-start.1 = (bf16[256,8192]{1,0:T(8,128)(2,1)S(1)}, bf16[256,8192]{1,0:T(8,128)(2,1)}, u32[]{:S(2)}) copy-start(bf16[256,8192]{1,0:T(8,128)(2,1)} %all-gather.9.cloned.1.call-done) | copy-start | bytes 12582916
  403.7 10.6 %copy-start.15 = (f32[256]{0:T(256)}, f32[256]{0:T(256)S(1)}, u32[]{:S(2)}) copy-start(f32[256]{0:T(256)S(1)} %get-tuple-element.15) | copy-start | bytes 3076
  408.0 10.5 %copy-start.5 = (bf16[256,128]{0,1:T(8,128)(2,1)}, bf16[256,128]{0,1:T(8,128)(2,1)S(1)}, u32[]{:S(2)}) copy-start(bf16[256,128]{0,1:T(8,128)(2,1)S(1)} %fusion.22) | copy-start | bytes 196612
  408.0 7.0 collective-permute-start
  414.5 3.9 copy-start.8
  415.0 3.8 copy-start.9
  423.0 7.2 collective-permute-start.1
  424.2 6.0 copy-start.7
  424.2 6.3 copy-start.2
  424.2 6.3 copy-start.12
  430.6 5.3 copy-start.14
  430.6 5.3 copy-start.16
  435.9 6.2 copy-start.6
  435.9 6.2 copy-start.10
  441.8 160.5 %reduce-scatter.4.cloned.1.call-start = ((), (), s32[]{:S(2)}) async-start(), calls=%async_computation.7 | async-start | bytes 4456448 | tf_op jit(solution)/shard_map/reduce_scatter | solution.py:126
  442.4 76.0 %copy-start.4 = (bf16[256,512]{1,0:T(8,128)(2,1)S(1)}, bf16[256,512]{1,0:T(8,128)(2,1)}, u32[]{:S(2)}) copy-start(bf16[256,512]{1,0:T(8,128)(2,1)} %param.17) | copy-start | bytes 786436
  450.2 152.0 %copy-start.3 = (bf16[256,512]{1,0:T(8,128)(2,1)S(1)}, bf16[256,512]{1,0:T(8,128)(2,1)}, u32[]{:S(2)}) copy-start(bf16[256,512]{1,0:T(8,128)(2,1)} %convolution_convert_fusion.4) | copy-start | bytes 786436
  450.2 323.8 %reduce-scatter.8.cloned.1.call-start = ((), (), s32[]{:S(2)}) async-start(), calls=%async_computation.10 | async-start | bytes 9437184 | tf_op jit(solution)/shard_map/reduce_scatter | solution.py:180
Sparse Core Ops, SparseCore 0:
  10.5 59.0 all-gather.4
  71.2 210.5 all-gather.6
  284.2 58.3 all-gather.10
  345.3 54.5 all-gather.8
  441.9 76.4 reduce-scatter.5
  522.8 79.4 reduce-scatter.3
  604.6 169.3 reduce-scatter.7
where the time goes:
time: 784 us
  waiting for transfers between devices  560 us (71%)
  blocking collectives  98.4 us (13%)
  matrix products  56.8 us (7%)
  local copies, waits for them, and re-layouts  30.8 us (4%)
  other arithmetic  21.2 us (3%)
  between operations  14.5 us (2%)
    reduce_scatter x1, waiting for transfers between devices, body(): lax.psum_scatter(lax.dot_general(features, grad_hidden, (((0,), (0,)), ((...  170 us
    all_to_all x1, blocking collectives, body(): lax.all_to_all(column_block, 'tok', split_axis=0, concat_axis=1, tiled=True)  98.4 us
    all_gather x1, waiting for transfers between devices, body(): lax.all_gather(stitch_weight, 'tok', axis=0, tiled=True)  91.1 us
    reduce_scatter x1, waiting for transfers between devices, body(): lax.psum_scatter(jnp.dot(context, o_weight, preferred_element_type=jnp.fl...  76 us
    reduce_scatter x1, waiting for transfers between devices, body(): lax.psum_scatter(norm_term.astype(jnp.bfloat16), 'tp', scatter_dimension=...  68.1 us
    all_gather x1, waiting for transfers between devices, body(): gradient_every_row = lax.all_gather(out_grad, 'tp', axis=1, tiled=True)  51.5 us
    all_gather x1, waiting for transfers between devices, body(): gathered = lax.all_gather(source, 'tp', axis=0, tiled=True)  51.3 us
    all_gather x1, waiting for transfers between devices, body(): hidden_all = lax.all_gather(hidden_bf, 'tp', axis=1, tiled=True)  49.4 us
  transfers between devices with their start and end apart: 9, of which 7 were waited for; matrix products, arithmetic and copies ran while one was open for 10% of the time, Pallas kernels for 0%

commit v1 on v0

--- a/solution.py
+++ b/solution.py
@@ -67,11 +67,13 @@
     column_block = jnp.take(gathered, placing, axis=0)
     token_rows = lax.all_to_all(column_block, "tok", split_axis=0, concat_axis=1, tiled=True)
     features = token_rows
-    hidden_cols = jnp.dot(
-        features,
-        lax.all_gather(stitch_weight, "tok", axis=0, tiled=True),
-        preferred_element_type=jnp.float32,
-    )
+
+    def bind_view(u_in):
+        return jnp.concatenate(
+            lax.all_to_all(jnp.stack(lax.axis_size("tok") * [u_in], 0), "tok", 0, 0), 0
+        )
+
+    hidden_cols = jnp.dot(features, bind_view(stitch_weight), preferred_element_type=jnp.float32)
     hidden_bf = hidden_cols.astype(jnp.bfloat16)
     hidden_all = lax.all_gather(hidden_bf, "tp", axis=1, tiled=True)
     hidden_f = hidden_all.astype(jnp.float32)

time: 784 us -> 641 us (0.82)
  waiting for transfers between devices: 560 us -> 453 us
  blocking collectives: 98.4 us -> 48.5 us
    all_gather x1 -> x0, waiting for transfers between devices: 91.1 us -> none  [body(): lax.all_gather(stitch_weight, 'tok', axis=0, tiled=True)]
    all_gather x1, waiting for transfers between devices: 51.5 us -> 0.01 us  [body(): gradient_every_row = lax.all_gather(out_grad, 'tp', axis=1, tiled=True)]
    all_to_all x1, blocking collectives: 98.4 us -> 48.5 us  [body(): lax.all_to_all(column_block, 'tok', split_axis=0, concat_axis=1, tiled=True)]
    all_to_all x0 -> x1, waiting for transfers between devices: none -> 33.6 us  [bind_view(): lax.all_to_all(jnp.stack(lax.axis_size('tok') * [u_in], 0), 'tok', 0, 0)]
    gather x2 -> x1, local copies, waits for them, and re-layouts: 20.1 us -> 13.7 us  [body(): column_block = jnp.take(gathered, placing, axis=0)]
  transfers between devices with their start and end apart: 9 -> 9, of which waited for: 7 -> 6; matrix products, arithmetic and copies ran while one was open for 10% -> 13% of each run, Pallas kernels for 0% -> 0%
where the time goes in v1:
time: 641 us; the launch traced here: 640 us
  waiting for transfers between devices  453 us (71%)
  matrix products  55.6 us (9%)
  blocking collectives  48.5 us (8%)
  local copies, waits for them, and re-layouts  38.3 us (6%)
  other arithmetic  21.7 us (3%)
  between operations  14.5 us (2%)
  starting transfers between devices  8.28 us (1%)
    reduce_scatter x1, waiting for transfers between devices, body(): lax.psum_scatter(lax.dot_general(features, grad_hidden, (((0,), (0,)), ((...  170 us
    reduce_scatter x1, waiting for transfers between devices, body(): lax.psum_scatter(jnp.dot(context, o_weight, preferred_element_type=jnp.fl...  75.9 us
    reduce_scatter x1, waiting for transfers between devices, body(): lax.psum_scatter(norm_term.astype(jnp.bfloat16), 'tp', scatter_dimension=...  61.5 us
    all_gather x1, waiting for transfers between devices, body(): gathered = lax.all_gather(source, 'tp', axis=0, tiled=True)  55.8 us
    all_gather x1, waiting for transfers between devices, body(): hidden_all = lax.all_gather(hidden_bf, 'tp', axis=1, tiled=True)  54.8 us
    all_to_all x1, blocking collectives, body(): lax.all_to_all(column_block, 'tok', split_axis=0, concat_axis=1, tiled=True)  48.5 us
    all_to_all x1, waiting for transfers between devices, bind_view(): lax.all_to_all(jnp.stack(lax.axis_size('tok') * [u_in], 0), 'tok', 0, 0)  33.6 us
    gather x1, local copies, waits for them, and re-layouts, body(): column_block = jnp.take(gathered, placing, axis=0)  13.7 us
  transfers between devices with their start and end apart: 9, of which 6 were waited for; matrix products, arithmetic and copies ran while one was open for 13% of the time, Pallas kernels for 0%

profile of v1, /device:TPU:1, one launch (start us, length us, event | category | flops | bytes accessed | tf_op | source)
XLA Modules:
  0.0 639.8 jit_solution(16818871389346440461)
XLA Ops:
  7.2 0.0 copy-start
  7.2 0.0 all-gather.4.cloned.1.call-start
  7.2 0.7 all-gather.4.cloned.1.call-update
  7.9 5.2 stack.2
  13.1 6.1 all-to-all-start.1
  19.2 0.0 all-gather.8.cloned.1.call-start
  19.2 0.7 all-gather.8.cloned.1.call-update
  19.9 0.0 all-gather.6.cloned.1.call-start
  20.0 8.0 %scatter_custom_fusion = s32[2048]{0:T(1024)S(1)} fusion(s32[2048]{0:T(1024)S(1)} %compare_select_fusion.1, s32[2048]{0:T(1024)S(1)} %iota.19, s32[]{:T(128)} %constant.22.clone.1), kind=kCustom, calls=%fused_computation.85 | custom fusion | bytes 8196 | tf_op jit(solution)/shard_map/scatter | solution.py:65
  28.1 55.8 %all-gather.4.cloned.1.call-done = bf16[2048,1024]{1,0:T(8,128)(2,1)} async-done(((bf16[128,1024]{1,0:T(8,128)(2,1)}), bf16[2048,1024]{1,0:T(8,128)(2,1)}) %all-gather.4.cloned.1.call-update) | async-done | bytes 4194320 | tf_op jit(solution)/shard_map/all_gather | solution.py:60
  83.9 13.7 %gather_fusion = bf16[2048,1024]{1,0:T(8,128)(2,1)} fusion(bf16[2048,1024]{1,0:T(8,128)(2,1)} %all-gather.4.cloned.1.call-done, s32[2048]{0:T(1024)S(1)} %fusion.44), kind=kCustom, calls=%fused_computation | custom fusion | bytes 8396800 | tf_op jit(solution)/shard_map/jit(_take)/gather | solution.py:67
  97.6 3.9 broadcast_select_fusion
  101.5 33.6 %all-to-all-done.1 = bf16[8,1024,512]{2,1,0:T(8,128)(2,1)} async-done(((bf16[8,1024,512]{2,1,0:T(8,128)(2,1)}), bf16[8,1024,512]{2,1,0:T(8,128)(2,1)}, u32[]{:S(2)}, u32[]{:S(2)}) %all-to-all-start.1) | async-done | bytes 8388640 | tf_op jit(solution)/shard_map/all_to_all | solution.py:73
  135.1 48.5 %all_to_all.21 = bf16[8,256,1024]{2,1,0:T(8,128)(2,1)S(1)} all-to-all(bf16[8,256,1024]{2,1,0:T(8,128)(2,1)} %broadcast_select_fusion), channel_id=1, replica_groups=mesh['tok'=8,'tp'=16] {'tok'}, dimensions={0} | all-to-all | bytes 8388608 | tf_op jit(solution)/shard_map/all_to_all | solution.py:68
  183.6 2.0 copy-done.3
  185.6 6.4 %fusion.10 = bf16[256,512]{1,0:T(8,128)(2,1)} fusion(bf16[8,1024,512]{2,1,0:T(8,128)(2,1)} %all-to-all-done.1, bf16[8,256,1024]{2,1,0:T(8,128)(2,1)S(1)} %all_to_all.21), kind=kOutput, calls=%fused_computation.25 | convolution fusion | flops 2147614720 | bytes 12845056 | tf_op jit(solution)/shard_map/dot_general | solution.py:76
  192.0 0.0 all-gather.6.cloned.1.call-update
  192.0 0.0 reduce-scatter.6.cloned.1.call-start
  192.1 0.1 convert_reduce_fusion
  192.2 0.3 multiply_cosine_fusion
  192.5 0.1 copy.28
  192.6 0.1 copy.26
  192.7 0.7 convert_compare_fusion
  193.5 7.0 %convolution_convert_fusion.3 = bf16[256,512]{1,0:T(8,128)(2,1)S(1)} fusion(bf16[256,8192]{1,0:T(8,128)(2,1)} %all-gather.8.cloned.1.call-done, bf16[512,8192]{1,0:T(8,128)(2,1)} %param.16), kind=kOutput, calls=%fused_computation.26 | convolution fusion | flops 2147614720 | bytes 12845056 | tf_op jit(solution)/shard_map/dot_general | solution.py:136
  200.5 0.8 copy.53
  201.4 54.8 %all-gather.6.cloned.1.call-done = bf16[256,8192]{1,0:T(8,128)(2,1)} async-done(((bf16[256,512]{1,0:T(8,128)(2,1)}), bf16[256,8192]{1,0:T(8,128)(2,1)}) %all-gather.6.cloned.1.call-update) | async-done | bytes 4194320 | tf_op jit(solution)/shard_map/all_gather | solution.py:78
  256.1 3.3 fusion.1
  259.4 0.6 multiply_multiply_fusion
  259.9 3.9 fusion.13
  263.9 0.3 fusion.33
  264.2 0.5 collective-permute-start
  264.8 5.8 fusion.11
  270.6 0.2 reshape.196
  270.8 0.3 fusion.53
  271.1 0.1 subtract_convert_fusion.1
  271.3 1.3 fusion.54
  272.6 0.2 fusion.16
  272.8 1.9 convolution_bitcast_fusion.3
  274.7 0.3 multiply_reduce_fusion
  275.1 0.3 fusion.17
  275.4 0.4 convolution_bitcast_fusion.4
  275.8 1.2 convolution_bitcast_fusion.1
  277.0 0.3 add_convert_fusion.1
  277.3 0.9 pad_maximum_fusion.1
  278.1 1.1 copy.36
  279.2 1.2 collective-permute-start.1
  280.5 5.9 fusion.55
  286.5 0.3 fusion.35
  286.8 5.3 fusion.7
  292.2 5.9 fusion.6
  298.0 0.0 reduce-scatter.6.cloned.1.call-update
  298.0 0.3 reduce-scatter.4.cloned.1.call-start
  298.3 0.3 convolution_convert_fusion.2
  298.7 7.7 %convolution_convert_fusion.1 = bf16[256,8192]{1,0:T(8,128)(2,1)} fusion(bf16[256,512]{0,1:T(8,128)(2,1)S(1)} %bitcast.91, bf16[512,8192]{1,0:T(8,128)(2,1)} %param.16), kind=kOutput, calls=%fused_computation.9 | convolution fusion | flops 2149580800 | bytes 12845056 | tf_op jit(solution)/shard_map/dot_general | solution.py:129
  306.4 0.0 reduce-scatter.4.cloned.1.call-update
  306.4 0.0 reduce-scatter.8.cloned.1.call-start
  306.5 6.6 %copy.31 = bf16[256,8,1024]{0,2,1:T(8,128)(2,1)} copy(bf16[256,8,1024]{2,0,1:T(8,128)(2,1)} %bitcast.89) | data formatting | bytes 8388608 | tf_op jit(solution)/shard_map/all_to_all | solution.py:68
  313.1 61.5 %reduce-scatter.6.cloned.1.call-done = bf16[256,512]{1,0:T(8,128)(2,1)} async-done(((bf16[256,8192]{1,0:T(8,128)(2,1)}), bf16[256,512]{1,0:T(8,128)(2,1)}) %reduce-scatter.6.cloned.1.call-update) | async-done | bytes 262160 | tf_op jit(solution)/shard_map/reduce_scatter | solution.py:177
  374.6 7.9 %convolution_convert_fusion = bf16[8192,512]{1,0:T(8,128)(2,1)} fusion(bf16[256,8192]{0,1:T(8,128)(2,1)} %bitcast.87, bf16[256,512]{1,0:T(8,128)(2,1)} %reduce-scatter.6.cloned.1.call-done, bf16[256,512]{1,0:T(8,128)(2,1)S(1)} %copy-done.4), kind=kOutput, calls=%fused_computation.6 | convolution fusion | flops 2152202240 | bytes 13107200 | tf_op jit(solution)/shard_map/dot_general | solution.py:183
  382.5 0.0 reduce-scatter.8.cloned.1.call-update
  382.6 75.9 %reduce-scatter.4.cloned.1.call-done = bf16[256,512]{1,0:T(8,128)(2,1)} async-done(((bf16[256,8192]{1,0:T(8,128)(2,1)}), bf16[256,512]{1,0:T(8,128)(2,1)}) %reduce-scatter.4.cloned.1.call-update) | async-done | bytes 262160 | tf_op jit(solution)/shard_map/reduce_scatter | solution.py:128
  458.5 1.7 add_convert_fusion.2
  460.2 169.9 %reduce-scatter.8.cloned.1.call-done = bf16[1024,512]{1,0:T(8,128)(2,1)} async-done(((bf16[8192,512]{1,0:T(8,128)(2,1)}), bf16[1024,512]{1,0:T(8,128)(2,1)}) %reduce-scatter.8.cloned.1.call-update) | async-done | bytes 1048592 | tf_op jit(solution)/shard_map/reduce_scatter | solution.py:182
  630.1 2.8 convert_element_type.137
  (50 shorter events, 0.2 us)
Async XLA Ops:
  7.2 252.8 %copy-start = (bf16[8192,128]{1,0:T(8,128)(2,1)S(1)}, bf16[8192,128]{1,0:T(8,128)(2,1)}, u32[]{:S(2)}) copy-start(bf16[8192,128]{1,0:T(8,128)(2,1)} %param.15) | copy-start | bytes 6291460
  7.2 76.7 %all-gather.4.cloned.1.call-start = ((), (), s32[]{:S(2)}) async-start(), calls=%async_computation.5 | async-start | bytes 4456448 | tf_op jit(solution)/shard_map/all_gather | solution.py:60
  13.1 6.9 %copy-start.15 = (s32[2048]{0:T(1024)S(1)}, s32[2048]{0:T(1024)}, u32[]{:S(2)}) copy-start(s32[2048]{0:T(1024)} %param.10) | copy-start | bytes 24580
  13.1 122.0 %all-to-all-start.1 = ((bf16[8,1024,512]{2,1,0:T(8,128)(2,1)}), bf16[8,1024,512]{2,1,0:T(8,128)(2,1)}, u32[]{:S(2)}, u32[]{:S(2)}) async-start(bf16[8,1024,512]{2,1,0:T(8,128)(2,1)} %stack.2), calls=%async_computation.1 | async-start | bytes 16777216 | tf_op jit(solution)/shard_map/all_to_all | solution.py:73
  19.2 174.3 %all-gather.8.cloned.1.call-start = ((), (), s32[]{:S(2)}) async-start(), calls=%async_computation.8 | async-start | bytes 4456448 | tf_op jit(solution)/shard_map/all_gather | solution.py:135
  19.9 236.2 %all-gather.6.cloned.1.call-start = ((), (), s32[]{:S(2)}) async-start(), calls=%async_computation.6 | async-start | bytes 4456448 | tf_op jit(solution)/shard_map/all_gather | solution.py:78
  183.6 2.0 copy-start.3
  185.6 6.5 %copy-start.14 = (s32[1,256]{1,0:T(1,128)S(1)}, s32[1,256]{1,0:T(1,128)}, u32[]{:S(2)}) copy-start(s32[1,256]{1,0:T(1,128)} %param.11) | copy-start | bytes 3076
  192.0 182.6 %reduce-scatter.6.cloned.1.call-start = ((), (), s32[]{:S(2)}) async-start(), calls=%async_computation.9 | async-start | bytes 4456448 | tf_op jit(solution)/shard_map/reduce_scatter | solution.py:177
  193.5 66.5 %copy-start.12 = (f32[8192]{0:T(1024)S(1)}, f32[8192]{0:T(1024)}, u32[]{:S(2)}) copy-start(f32[8192]{0:T(1024)} %param.13) | copy-start | bytes 98308
  256.1 8.6 %copy-start.1 = (bf16[256,8192]{1,0:T(8,128)(2,1)S(1)}, bf16[256,8192]{1,0:T(8,128)(2,1)}, u32[]{:S(2)}) copy-start(bf16[256,8192]{1,0:T(8,128)(2,1)} %all-gather.6.cloned.1.call-done) | copy-start | bytes 12582916
  259.9 10.7 %copy-start.17 = (f32[256]{0:T(256)}, f32[256]{0:T(256)S(1)}, u32[]{:S(2)}) copy-start(f32[256]{0:T(256)S(1)} %get-tuple-element.15) | copy-start | bytes 3076
  264.2 10.5 %copy-start.6 = (bf16[256,128]{0,1:T(8,128)(2,1)}, bf16[256,128]{0,1:T(8,128)(2,1)S(1)}, u32[]{:S(2)}) copy-start(bf16[256,128]{0,1:T(8,128)(2,1)S(1)} %fusion.23) | copy-start | bytes 196612
  264.2 7.1 %collective-permute-start = (bf16[256,128]{0,1:T(8,128)(2,1)S(1)}, bf16[256,128]{0,1:T(8,128)(2,1)S(1)}, u32[]{:S(2)}, u32[]{:S(2)}) collective-permute-start(bf16[256,128]{0,1:T(8,128)(2,1)S(1)} %fusion.23), channel_id=1, source_target_pairs={{0,1},{1,0},{2,3},{3,2},{4,5},{5,4},{6,7},{7,6},{8,9},{9,8},{10,11... | collective-permute-start | bytes 196616 | tf_op jit(solution)/shard_map/ppermute | solution.py:14
  270.8 3.9 copy-start.9
  271.3 3.8 copy-start.10
  279.2 7.2 %collective-permute-start.1 = (bf16[256,128]{0,1:T(8,128)(2,1)S(1)}, bf16[256,128]{0,1:T(8,128)(2,1)S(1)}, u32[]{:S(2)}, u32[]{:S(2)}) collective-permute-start(bf16[256,128]{0,1:T(8,128)(2,1)S(1)} %fusion.37), channel_id=1, source_target_pairs={{0,1},{1,0},{2,3},{3,2},{4,5},{5,4},{6,7},{7,6},{8,9},{9,8},{10,11... | collective-permute-start | bytes 196616 | tf_op jit(solution)/shard_map/ppermute | solution.py:14
  280.5 6.0 copy-start.8
  280.5 6.3 copy-start.2
  280.5 6.3 copy-start.13
  286.8 5.3 copy-start.16
  286.8 5.3 copy-start.18
  292.1 6.2 copy-start.7
  292.2 6.2 copy-start.11
  298.0 160.5 %reduce-scatter.4.cloned.1.call-start = ((), (), s32[]{:S(2)}) async-start(), calls=%async_computation.7 | async-start | bytes 4456448 | tf_op jit(solution)/shard_map/reduce_scatter | solution.py:128
  306.4 68.3 %copy-start.4 = (bf16[256,512]{1,0:T(8,128)(2,1)S(1)}, bf16[256,512]{1,0:T(8,128)(2,1)}, u32[]{:S(2)}) copy-start(bf16[256,512]{1,0:T(8,128)(2,1)} %param.17) | copy-start | bytes 786436
  306.4 323.7 %reduce-scatter.8.cloned.1.call-start = ((), (), s32[]{:S(2)}) async-start(), calls=%async_computation.10 | async-start | bytes 9437184 | tf_op jit(solution)/shard_map/reduce_scatter | solution.py:182
  374.6 83.9 %copy-start.5 = (bf16[256,512]{1,0:T(8,128)(2,1)S(1)}, bf16[256,512]{1,0:T(8,128)(2,1)}, u32[]{:S(2)}) copy-start(bf16[256,512]{1,0:T(8,128)(2,1)} %fusion.10) | copy-start | bytes 786436
Sparse Core Ops, SparseCore 0:
  10.5 73.3 all-gather.3
  86.3 66.0 all-gather.7
  192.1 63.9 all-gather.5
  298.2 76.4 reduce-scatter.5
  379.0 79.4 reduce-scatter.3
  460.8 169.3 reduce-scatter.7
